TPU v7x, 32 devices: a whole 2x2x4 slice. The times are simulated.
32 devices in a mesh: gx: 2 (over x), gy: 16 (over z, y, core).
Axes of the slice: x: 2, y: 2, z: 4, core: 2. Of those that a mesh axis runs over, the one named last changes fastest.
Arguments:
- density: float32 [1, 2048, 2048], P(None, 'gy', 'gx'), may hold values from 0.35 to 2.5, as said below
- xmomentum: float32 [1, 2048, 2048], P(None, 'gy', 'gx'), may hold values from -2.5 to 2.5
- ymomentum: float32 [1, 2048, 2048], P(None, 'gy', 'gx'), may hold values from -2.5 to 2.5
- shear_shift: int32 [1], replicated, may hold values from 0 to 2047
Outputs:
- density_new: float32 [1, 2048, 2048], P(None, 'gy', 'gx')
- xmomentum_new: float32 [1, 2048, 2048], P(None, 'gy', 'gx')
- ymomentum_new: float32 [1, 2048, 2048], P(None, 'gy', 'gx')
- potential: float32 [1, 2048, 2048], P(None, 'gy', 'gx')
Inputs may be any that keep to these rules, and one draw needn't show every extreme that they name: Every density is positive.
All inputs are finite; a program needn't handle non-finite values.
Results may differ from a plain program's by a relative error of at most 0.00065.
Values sent between devices are 32-bit elements; how exact they have to be, the bound alone decides.
A program may use at most 64 MiB of HBM per device.

v0:
```python
import functools

import jax
import jax.numpy as jnp
import ml_dtypes
import numpy as np
from jax import lax
from jax.experimental import pallas as pl
from jax.experimental.pallas import tpu as pltpu
from jax.sharding import PartitionSpec as P

sound_speed = 1.0
time_step = 0.15
omega_rate = 0.5
shear_rate = 1.5
thickness = 0.5

LANES = 128
MESH = pl.DeviceIdType.MESH
VMEM = pl.BlockSpec(memory_space=pltpu.VMEM)


def split_np(table):
    head = table.astype(np.float32).astype(ml_dtypes.bfloat16)
    tail = (table - head.astype(np.float64)).astype(np.float32).astype(ml_dtypes.bfloat16)
    return np.stack([head, tail])


def split(value):
    head = value.astype(jnp.bfloat16)
    return head, (value - head.astype(jnp.float32)).astype(jnp.bfloat16)


def dot3(left, right, dims):
    def one(a, b):
        return lax.dot_general(a, b, (dims, ((), ())), preferred_element_type=jnp.float32)

    return one(left[0], right[0]) + (one(left[0], right[1]) + one(left[1], right[0]))


def exchange_kernel(count, gy, whole, src, dst, send, recv, own):
    radial = lax.axis_index("gx")
    azimuth = lax.axis_index("gy")
    me = radial * gy + azimuth if whole else azimuth

    def place(step):
        peer = lax.rem(me + step, count)
        device = (lax.div(peer, gy), lax.rem(peer, gy)) if whole else (radial, peer)
        return peer, device

    barrier = pltpu.get_barrier_semaphore()

    def greet(step, _):
        pl.semaphore_signal(barrier, inc=1, device_id=place(step)[1], device_id_type=MESH)
        return _

    def copy(step):
        peer, device = place(step)
        return pltpu.make_async_remote_copy(
            src_ref=src.at[peer],
            dst_ref=dst.at[me],
            send_sem=send.at[step],
            recv_sem=recv.at[step],
            device_id=device,
            device_id_type=MESH,
        )

    def start(step, _):
        copy(step).start()
        return _

    def finish(step, _):
        copy(step).wait()
        return _

    lax.fori_loop(1, count, greet, 0)
    mine = pltpu.make_async_copy(src.at[me], dst.at[me], own)
    mine.start()
    pl.semaphore_wait(barrier, count - 1)
    lax.fori_loop(1, count, start, 0)
    mine.wait()
    lax.fori_loop(1, count, finish, 0)


def exchange(blocks, gy, whole, ident):
    count = blocks.shape[0]
    return pl.pallas_call(
        functools.partial(exchange_kernel, count, gy, whole),
        out_shape=jax.ShapeDtypeStruct(blocks.shape, blocks.dtype),
        in_specs=[VMEM],
        out_specs=VMEM,
        scratch_shapes=[
            pltpu.SemaphoreType.DMA((count,)),
            pltpu.SemaphoreType.DMA((count,)),
            pltpu.SemaphoreType.DMA,
        ],
        compiler_params=pltpu.CompilerParams(collective_id=ident, has_side_effects=True),
    )(blocks)


def halo_kernel(gx, gy, d_ref, x_ref, y_ref, cols, rows, colbuf, rowbuf, csend, crecv, rsend, rrecv):
    radial = lax.axis_index("gx")
    azimuth = lax.axis_index("gy")
    before = lax.rem(radial + gx - 1, gx)
    after = lax.rem(radial + 1, gx)
    below = lax.rem(azimuth + gy - 1, gy)
    above = lax.rem(azimuth + 1, gy)
    height, width = d_ref.shape
    barrier = pltpu.get_barrier_semaphore()

    def greet(step, _):
        there = lax.rem(azimuth + step, gy)
        pl.semaphore_signal(barrier, inc=1, device_id=(before, there), device_id_type=MESH)
        pl.semaphore_signal(barrier, inc=1, device_id=(after, there), device_id_type=MESH)
        return _

    lax.fori_loop(0, gy, greet, 0)
    pl.semaphore_signal(barrier, inc=1, device_id=(radial, below), device_id_type=MESH)
    pl.semaphore_signal(barrier, inc=1, device_id=(radial, above), device_id_type=MESH)
    rowbuf[...] = jnp.zeros_like(rowbuf)
    colbuf[...] = jnp.zeros_like(colbuf)
    for at, ref in enumerate((d_ref, x_ref, y_ref)):
        rowbuf[0, at : at + 1, :] = ref[0:1, :]
        rowbuf[1, at : at + 1, :] = ref[height - 1 : height, :]
        colbuf[0, at : at + 1, :] = ref[:, 0:LANES].T[0:1, :]
        colbuf[1, at : at + 1, :] = ref[:, width - LANES : width].T[LANES - 1 : LANES, :]
    pl.semaphore_wait(barrier, 2 * gy + 2)

    def row_copy(side):
        return pltpu.make_async_remote_copy(
            src_ref=rowbuf.at[side],
            dst_ref=rows.at[1 - side],
            send_sem=rsend.at[side],
            recv_sem=rrecv.at[side],
            device_id=(radial, below if side == 0 else above),
            device_id_type=MESH,
        )

    def col_copy(side, step):
        there = lax.rem(azimuth + step, gy)
        return pltpu.make_async_remote_copy(
            src_ref=colbuf.at[side],
            dst_ref=cols.at[1 - side, azimuth],
            send_sem=csend.at[side, step],
            recv_sem=crecv.at[side, step],
            device_id=(before if side == 0 else after, there),
            device_id_type=MESH,
        )

    def start(step, _):
        col_copy(0, step).start()
        col_copy(1, step).start()
        return _

    def finish(step, _):
        col_copy(0, step).wait()
        col_copy(1, step).wait()
        return _

    row_copy(0).start()
    row_copy(1).start()
    lax.fori_loop(0, gy, start, 0)
    row_copy(0).wait()
    row_copy(1).wait()
    lax.fori_loop(0, gy, finish, 0)


def halo(fields, gx, gy, ident):
    height, width = fields[0].shape
    return pl.pallas_call(
        functools.partial(halo_kernel, gx, gy),
        out_shape=(
            jax.ShapeDtypeStruct((2, gy, 8, height), jnp.float32),
            jax.ShapeDtypeStruct((2, 8, width), jnp.float32),
        ),
        in_specs=[VMEM] * 3,
        out_specs=(VMEM, VMEM),
        scratch_shapes=[
            pltpu.VMEM((2, 8, height), jnp.float32),
            pltpu.VMEM((2, 8, width), jnp.float32),
            pltpu.SemaphoreType.DMA((2, gy)),
            pltpu.SemaphoreType.DMA((2, gy)),
            pltpu.SemaphoreType.DMA((2,)),
            pltpu.SemaphoreType.DMA((2,)),
        ],
        compiler_params=pltpu.CompilerParams(collective_id=ident, has_side_effects=True),
    )(*fields)


def flux_of(state, normal):
    velocity = state[normal] / state[0]
    parts = [state[0] * velocity, state[1] * velocity, state[2] * velocity]
    parts[normal] = parts[normal] + sound_speed * sound_speed * state[0]
    return parts, jnp.abs(velocity)


def rusanov(left, right, left_flux, right_flux, left_speed, right_speed):
    speed = jnp.maximum(left_speed, right_speed) + sound_speed
    return [
        0.5 * (fl + fr) - 0.5 * speed * (r - l)
        for l, r, fl, fr in zip(left, right, left_flux, right_flux)
    ]


def gas_update(now, down, up, west, east):
    change = [None] * 3
    for low, high, normal in ((west, east, 1), (down, up, 2)):
        low_f, low_s = flux_of(low, normal)
        mid_f, mid_s = flux_of(now, normal)
        high_f, high_s = flux_of(high, normal)
        left = rusanov(low, now, low_f, mid_f, low_s, mid_s)
        right = rusanov(now, high, mid_f, high_f, mid_s, high_s)
        for f in range(3):
            term = right[f] - left[f]
            change[f] = term if change[f] is None else change[f] + term
    return (
        now[0] - time_step * change[0],
        now[1] - time_step * change[1] + time_step * 2.0 * omega_rate * now[2],
        now[2] - time_step * change[2] - time_step * (2.0 - shear_rate) * omega_rate * now[1],
    )


def gas_kernel(d_ref, x_ref, y_ref, rows, cols, d_out, x_out, y_out):
    height, width = d_ref.shape
    refs = (d_ref, x_ref, y_ref)
    blocks = height // 8
    ghost = cols[...]
    ghost = jnp.concatenate([ghost[0], ghost[1]], axis=0).T
    sub = lax.broadcasted_iota(jnp.int32, (8, width), 0)
    lane = lax.broadcasted_iota(jnp.int32, (8, width), 1)
    for block in range(blocks):
        at = block * 8
        now = [ref[at : at + 8, :] for ref in refs]
        sides = ghost[at : at + 8]
        down, up, west, east = [], [], [], []
        for f in range(3):
            edge = refs[f][at - 1 : at, :] if block else rows[0, f : f + 1, :]
            down.append(jnp.where(sub == 0, edge, pltpu.roll(now[f], 1, 0)))
            edge = refs[f][at + 8 : at + 9, :] if block < blocks - 1 else rows[1, f : f + 1, :]
            up.append(jnp.where(sub == 7, edge, pltpu.roll(now[f], 7, 0)))
            west.append(jnp.where(lane == 0, sides[:, f : f + 1], pltpu.roll(now[f], 1, 1)))
            east.append(
                jnp.where(lane == width - 1, sides[:, 8 + f : 9 + f], pltpu.roll(now[f], width - 1, 1))
            )
        fresh = gas_update(now, down, up, west, east)
        d_out[at : at + 8, :], x_out[at : at + 8, :], y_out[at : at + 8, :] = fresh


def gas(fields, rows, cols):
    shape = jax.ShapeDtypeStruct(fields[0].shape, jnp.float32)
    return pl.pallas_call(
        gas_kernel,
        out_shape=(shape, shape, shape),
        in_specs=[VMEM] * 5,
        out_specs=(VMEM, VMEM, VMEM),
    )(*fields, rows, cols)


def unpack_kernel(d_ref, x_ref, y_ref, src, d_out, x_out, y_out, out):
    d_out[...] = d_ref[...]
    x_out[...] = x_ref[...]
    y_out[...] = y_ref[...]
    gy, packed, _ = src.shape
    low = lax.broadcasted_iota(jnp.int32, (packed, LANES), 1) < LANES // 2
    for tile in range(gy // 2):
        span = slice(tile * LANES, (tile + 1) * LANES)
        near, far = src[2 * tile], src[2 * tile + 1]
        out[0:packed, span] = jnp.where(low, near, flip(far))
        out[packed : 2 * packed, span] = jnp.where(low, flip(near), far)


def unpack(fields, blocks):
    shape = jax.ShapeDtypeStruct(fields[0].shape, jnp.float32)
    return pl.pallas_call(
        unpack_kernel,
        out_shape=(shape,) * 4,
        in_specs=[VMEM] * 4,
        out_specs=(VMEM,) * 4,
    )(*fields, blocks)


def slot_wave(group, index, gy, height):
    half = height // 2
    first = jnp.where(index < half, gy * index, gy // 2 + gy * (index - half))
    return jnp.where(group == 0, first, group + gy * index)


def azimuth_table(gy, height):
    ny = gy * height
    b = np.arange(height)
    out = np.zeros((gy // 2, 2 * height, 2 * height))
    for group in range(1, gy // 2):
        m = group + gy * np.arange(height)
        angle = 2.0 * np.pi * ((m[:, None] * b[None, :]) % ny) / ny
        c, s = np.cos(angle), np.sin(angle)
        out[group] = np.block([[c, s], [-s, c]])
    half = height // 2
    for part, residue in enumerate((0, gy // 2)):
        m = residue + gy * np.arange(half)
        angle = 2.0 * np.pi * ((m[:, None] * b[None, :]) % ny) / ny
        c, s = np.cos(angle), -np.sin(angle)
        if part == 0:
            s[0] = 1.0 - 2.0 * (b % 2)
        out[0, part * half : (part + 1) * half, part * height : (part + 1) * height] = c
        out[0, height + part * half : height + (part + 1) * half, part * height : (part + 1) * height] = s
    return split_np(out)


def azimuth_kernel(xb, src, table, out, stage):
    gy, packed, _ = src.shape
    height = table.shape[2] // 2
    fold = height // packed
    lane = lax.broadcasted_iota(jnp.int32, (height, LANES), 1)
    half = gy // 2
    step = 8 if packed % 8 == 0 else packed

    def put(group, base, at, value):
        for h in range(fold):
            row = base + h * packed + at
            stage[group, row : row + step, :] = (
                value if h == 0 else pltpu.roll(value, LANES - h * xb, 1)
            )

    for at in range(0, packed, step):
        f = [src[a, at : at + step, :] for a in range(gy)]
        plus = [None] + [f[a] + f[gy - a] for a in range(1, half)]
        minus = [None] + [f[a] - f[gy - a] for a in range(1, half)]
        for g in range(half + 1):
            re = f[0] + f[half] if g % 2 == 0 else f[0] - f[half]
            im = None
            for a in range(1, half):
                re = re + float(np.cos(2.0 * np.pi * ((a * g) % gy) / gy)) * plus[a]
                if 0 < g < half:
                    term = float(-np.sin(2.0 * np.pi * ((a * g) % gy) / gy)) * minus[a]
                    im = term if im is None else im + term
            if g == half:
                put(0, height, at, re)
            else:
                put(g, 0, at, re)
                if g:
                    put(g, height, at, im)
    for g in range(half):
        both = dot3((table[0, g], table[1, g]), split(stage[g]), ((1,), (0,)))
        out[g] = jnp.where(lane < xb, both[:height], pltpu.roll(both[height:], xb, 1))


def azimuth_forward(blocks, table, xb):
    gy, packed, _ = blocks.shape
    height = table.shape[2] // 2
    return pl.pallas_call(
        functools.partial(azimuth_kernel, xb),
        out_shape=jax.ShapeDtypeStruct((gy // 2, height, LANES), jnp.float32),
        in_specs=[VMEM] * 2,
        out_specs=VMEM,
        scratch_shapes=[pltpu.VMEM((gy // 2, 2 * height, LANES), jnp.float32)],
    )(blocks, table)


def azimuth_back_kernel(xb, src, table, out, stage):
    gy, packed, _ = out.shape
    height = table.shape[2] // 2
    fold = height // packed
    half = gy // 2
    step = 8 if packed % 8 == 0 else packed
    lane = lax.broadcasted_iota(jnp.int32, (step, LANES), 1)
    for g in range(half):
        value = src[g]
        value = jnp.concatenate([value, pltpu.roll(value, LANES - xb, 1)], axis=0)
        stage[g] = dot3((table[0, g], table[1, g]), split(value), ((0,), (0,)))

    def take(group, base, at):
        total = None
        for h in range(fold):
            row = base + h * packed + at
            value = stage[group, row : row + step, :]
            value = value if h == 0 else pltpu.roll(value, h * xb, 1)
            total = value if h == 0 else jnp.where(lane < h * xb, total, value)
        return total

    for at in range(0, packed, step):
        re = [take(g, 0, at) for g in range(half)]
        im = [None] + [take(g, height, at) for g in range(1, half)]
        last = take(0, height, at)
        for a in range(half + 1):
            even = re[0] + last if a % 2 == 0 else re[0] - last
            odd = None
            for g in range(1, half):
                angle = 2.0 * np.pi * ((a * g) % gy) / gy
                even = even + float(np.cos(angle)) * re[g]
                if 0 < a < half:
                    term = float(np.sin(angle)) * im[g]
                    odd = term if odd is None else odd + term
            if odd is None:
                out[a, at : at + step, :] = even
            else:
                out[a, at : at + step, :] = even - odd
                out[gy - a, at : at + step, :] = even + odd


def azimuth_back(slots, table, xb, gy, packed):
    height = table.shape[2] // 2
    return pl.pallas_call(
        functools.partial(azimuth_back_kernel, xb),
        out_shape=jax.ShapeDtypeStruct((gy, packed, LANES), jnp.float32),
        in_specs=[VMEM] * 2,
        out_specs=VMEM,
        scratch_shapes=[pltpu.VMEM((gy // 2, 2 * height, LANES), jnp.float32)],
    )(slots, table)


def flip(value):
    return pltpu.roll(value, LANES // 2, value.ndim - 1)


def fft_packed(parts, sign, signs):
    count = len(parts)
    if count == 1:
        return parts
    even = fft_packed(parts[0::2], sign, signs)
    odd = fft_packed(parts[1::2], sign, signs)
    low, high = [], []
    for k in range(count // 2):
        value = odd[k]
        if k:
            angle = sign * 2.0 * np.pi * k / count
            turned = flip(value) * signs
            if 4 * k == count:
                value = turned * float(np.sin(angle))
            else:
                value = value * float(np.cos(angle)) + turned * float(np.sin(angle))
        low.append(even[k] + value)
        high.append(even[k] - value)
    return low + high


def radial_tables(nx):
    wide = LANES // 2
    outer = nx // wide
    j = np.arange(wide)
    angle = 2.0 * np.pi * (np.outer(np.arange(outer), j) % nx) / nx
    c, s = np.cos(angle), np.sin(angle)
    turn = np.stack([np.concatenate([c, c], 1), np.concatenate([s, -s], 1)])
    angle = 2.0 * np.pi * (np.outer(j, j) % wide) / wide
    c, s = np.cos(angle), np.sin(angle)
    return turn.astype(np.float32), split_np(np.block([[c, -s], [s, c]]))


def radial_kernel(nx, ny, lines, src, wave, sigma, outer_turn, inner_turn, turn, table, out, stage):
    outer = src.shape[0]
    padded = stage.shape[1]
    half = LANES // 2
    gy = lax.axis_size("gy")
    first = jnp.logical_and(lax.axis_index("gx") == 0, lax.axis_index("gy") == 0)
    keep = jnp.where(first, 0.0, 1.0)
    lane8 = lax.broadcasted_iota(jnp.int32, (8, LANES), 1)
    sub8 = lax.broadcasted_iota(jnp.int32, (8, LANES), 0)
    signs = jnp.where(lane8 < half, -1.0, 1.0)
    low = lane8 < half

    def load(d, at):
        if at + 8 <= lines:
            value = src[d, at : at + 8, :]
            if at == 0:
                value = jnp.where(jnp.logical_and(sub8 == 0, lane8 >= half), value * keep, value)
            return value
        top = src[d, 0:1, :]
        extra = jnp.where(low[0:1], flip(jnp.broadcast_to(top, (8, LANES)))[0:1], 0.0)
        if at >= lines:
            return jnp.where(sub8 == 0, extra, 0.0)
        body = jnp.concatenate([src[d, at:lines, :], jnp.zeros((8 - lines + at, LANES), jnp.float32)], 0)
        if at == 0:
            body = jnp.where(jnp.logical_and(sub8 == 0, lane8 >= half), body * keep, body)
        return jnp.where(sub8 == lines - at, extra, body)

    def turned(value, c, s):
        return value * c + flip(value) * s

    for at in range(0, padded, 8):
        ci, si = inner_turn[0, at : at + 8, :], inner_turn[1, at : at + 8, :]
        parts = []
        for d in range(outer):
            co = outer_turn[0, at : at + 8, d : d + 1]
            so = outer_turn[1, at : at + 8, d : d + 1]
            parts.append(turned(load(d, at), co, -so * signs))
        parts = fft_packed(parts, -1.0, signs)
        for n in range(outer):
            value = turned(parts[n], ci, -si * signs)
            stage[n, at : at + 8, :] = turned(value, turn[0, n : n + 1, :], turn[1, n : n + 1, :])

    column = lax.broadcasted_iota(jnp.int32, (padded, LANES), 1)
    column = jnp.where(column < half, column, column - half)
    m = jnp.broadcast_to(wave[:, 0:1], (padded, LANES))
    shear = jnp.broadcast_to(sigma[:, 0:1], (padded, LANES)).astype(jnp.float32) / ny
    signed = jnp.where(m < ny // 2, m, m - ny).astype(jnp.float32)
    wave_y = 2.0 * jnp.pi / ny * signed
    wave_y = wave_y * wave_y
    weight = jnp.where(jnp.logical_or(m == 0, m == ny // 2), 1.0, 2.0) / (nx * ny)

    def convolve(n, _):
        modes = dot3(split(stage[n]), (table[0], table[1]), ((1,), (0,)))
        x_wave = n + outer * column
        x_signed = jnp.where(x_wave < nx // 2, x_wave, x_wave - nx).astype(jnp.float32)
        wave_x = 2.0 * jnp.pi / nx * (x_signed + shear)
        magnitude = jnp.sqrt(wave_x * wave_x + wave_y)
        anchor = jnp.logical_and(m == 0, x_wave == 0)
        safe = jnp.where(anchor, 1.0, magnitude)
        green = jnp.where(anchor, 0.0, -jnp.exp(-thickness * safe) / safe)
        modes = modes * (green * weight)
        stage[n] = dot3(split(modes), (table[0], table[1]), ((1,), (1,)))
        return _

    lax.fori_loop(0, outer, convolve, 0)

    for at in range(0, lines, 8):
        high = min(at + 8, lines)
        ci, si = inner_turn[0, at : at + 8, :], inner_turn[1, at : at + 8, :]
        more = lines - lines % 8
        parts = []
        for n in range(outer):
            value = turned(stage[n, at : at + 8, :], turn[0, n : n + 1, :], -turn[1, n : n + 1, :])
            parts.append(turned(value, ci, si * signs))
        parts = fft_packed(parts, 1.0, signs)
        if at == 0:
            ce, se = inner_turn[0, more : more + 8, :], inner_turn[1, more : more + 8, :]
            extras = []
            for n in range(outer):
                value = turned(stage[n, more : more + 8, :], turn[0, n : n + 1, :], -turn[1, n : n + 1, :])
                extras.append(turned(value, ce, se * signs))
            extras = fft_packed(extras, 1.0, signs)
        for d in range(outer):
            co = outer_turn[0, at : at + 8, d : d + 1]
            so = outer_turn[1, at : at + 8, d : d + 1]
            value = turned(parts[d], co, so * signs)
            if at == 0:
                co = outer_turn[0, more : more + 8, d : d + 1]
                so = outer_turn[1, more : more + 8, d : d + 1]
                extra = flip(turned(extras[d], co, so * signs))[lines % 8 : lines % 8 + 1]
                mask = jnp.logical_and(jnp.logical_and(sub8 == 0, lane8 >= half), first)
                value = jnp.where(mask, extra, value)
            out[d, at:high, :] = value[: high - at]


def radial(blocks, wave, sigma, outer_turn, inner_turn, turn, table, nx, ny):
    outer, lines, _ = blocks.shape
    padded = wave.shape[0]
    return pl.pallas_call(
        functools.partial(radial_kernel, nx, ny, lines),
        out_shape=jax.ShapeDtypeStruct(blocks.shape, jnp.float32),
        in_specs=[VMEM] * 7,
        out_specs=VMEM,
        scratch_shapes=[pltpu.VMEM((outer, padded, LANES), jnp.float32)],
    )(blocks, wave, sigma, outer_turn, inner_turn, turn, table)


def modulo(value, size):
    return value & (size - 1) if size & (size - 1) == 0 else lax.rem(value, size)


def fused_kernel(
    nx, ny, shift_ref, d_ref, x_ref, y_ref, y_source, turn, x_table, d_final, x_final, y_final, out,
    d_out, x_out, y_out, y_table, table_sem, field_sem,
    cols, rows, colbuf, colbuf2, rowbuf, outer_turn, inner_turn, src,
    got1, stage, give2, got2, green, mid, extra, give3, got3, give4,
    csend, crecv, rsend, rrecv, send1, recv1, send2, recv2, send3, recv3, send4, recv4,
):
    gx, gy = lax.axis_size("gx"), lax.axis_size("gy")
    radial_at, azimuth = lax.axis_index("gx"), lax.axis_index("gy")
    count = gx * gy
    me = radial_at * gy + azimuth
    height, width = d_ref.shape
    packed = src.shape[1]
    half_gy = gy // 2
    outer, lines, _ = got2.shape
    padded = inner_turn.shape[1]
    wide = LANES // 2
    step1 = packed // 4
    parts2 = lines // 8
    first = me == 0
    keep = jnp.where(first, 0.0, 1.0)
    lane8 = lax.broadcasted_iota(jnp.int32, (8, LANES), 1)
    sub8 = lax.broadcasted_iota(jnp.int32, (8, LANES), 0)
    signs = jnp.where(lane8 < wide, -1.0, 1.0)
    low = lane8 < wide
    fields = (d_ref, x_ref, y_ref)
    fresh = (d_out, x_out, y_out)
    before = lax.rem(radial_at + gx - 1, gx)
    after = lax.rem(radial_at + 1, gx)
    below = lax.rem(azimuth + gy - 1, gy)
    above = lax.rem(azimuth + 1, gy)
    inner_edge = radial_at == 0
    outer_edge = radial_at == gx - 1

    def device_of(peer):
        return lax.div(peer, gy), lax.rem(peer, gy)

    table_load = pltpu.make_async_copy(y_source, y_table, table_sem)
    table_load.start()
    cols[...] = jnp.zeros_like(cols)
    barrier = pltpu.get_barrier_semaphore()

    def greet(k, _):
        there = device_of(lax.rem(me + k, count))
        pl.semaphore_signal(barrier, inc=1, device_id=there, device_id_type=MESH)
        return _

    lax.fori_loop(1, count, greet, 0)

    rowbuf[...] = jnp.zeros_like(rowbuf)
    colbuf[...] = jnp.zeros_like(colbuf)
    for at, ref in enumerate(fields):
        rowbuf[0, at : at + 1, :] = ref[0:1, :]
        rowbuf[1, at : at + 1, :] = ref[height - 1 : height, :]
        colbuf[0, at : at + 1, :] = ref[:, 0:LANES].T[0:1, :]
        colbuf[1, at : at + 1, :] = ref[:, width - LANES : width].T[LANES - 1 : LANES, :]

    def row_copy(side):
        return pltpu.make_async_remote_copy(
            src_ref=rowbuf.at[side],
            dst_ref=rows.at[1 - side],
            send_sem=rsend.at[side],
            recv_sem=rrecv.at[side],
            device_id=(radial_at, below if side == 0 else above),
            device_id_type=MESH,
        )

    def col_copy(side, k):
        return pltpu.make_async_remote_copy(
            src_ref=colbuf.at[side],
            dst_ref=cols.at[1 - side, azimuth],
            send_sem=csend.at[side, k],
            recv_sem=crecv.at[side, k],
            device_id=(before if side == 0 else after, lax.rem(azimuth + k, gy)),
            device_id_type=MESH,
        )

    outgoing = (jnp.where(inner_edge, gy, 1), jnp.where(outer_edge, gy, 1))
    incoming = (jnp.where(outer_edge, gy, 1), jnp.where(inner_edge, gy, 1))

    def col_each(side, peers, act):
        def body(k, _):
            act(col_copy(side, k))
            return _

        lax.fori_loop(0, peers, body, 0)

    def line_copy(give, got, send, recv, rows, part, k):
        peer = lax.rem(azimuth + k, gy)
        span = pl.ds(pl.multiple_of(part * rows, rows), rows)
        return pltpu.make_async_remote_copy(
            src_ref=give.at[peer, span],
            dst_ref=got.at[azimuth, span],
            send_sem=send.at[part, k],
            recv_sem=recv.at[part, k],
            device_id=(radial_at, peer),
            device_id_type=MESH,
        )

    def all_copy(give, got, send, recv, rows, part, k):
        peer = lax.rem(me + k, count)
        span = pl.ds(pl.multiple_of(part * rows, rows), rows)
        return pltpu.make_async_remote_copy(
            src_ref=give.at[peer, span],
            dst_ref=got.at[me, span],
            send_sem=send.at[part, k],
            recv_sem=recv.at[part, k],
            device_id=device_of(peer),
            device_id_type=MESH,
        )

    def each(copy, peers, act):
        def body(k, _):
            act(copy(k))
            return _

        lax.fori_loop(1, peers, body, 0)

    def start(c):
        c.start()

    def arrive(c):
        c.wait_recv()

    def leave(c):
        c.wait_send()

    one = functools.partial(line_copy, src, got1, send1, recv1, step1)
    two = functools.partial(all_copy, give2, got2, send2, recv2, 8)
    three = functools.partial(all_copy, give3, got3, send3, recv3, 8)
    four = functools.partial(line_copy, give4, out, send4, recv4, step1)

    pl.semaphore_wait(barrier, count - 1)
    for side in range(2):
        row_copy(side).start()
        col_each(side, outgoing[side], start)

    blocks = height // 8
    sub_wide = lax.broadcasted_iota(jnp.int32, (8, width), 0)
    lane_wide = lax.broadcasted_iota(jnp.int32, (8, width), 1)

    def inner_rows(block, _):
        span = pl.ds(pl.multiple_of(block * 8, 8), 8)
        span_down = pl.ds(pl.multiple_of(block * 8 - 8, 8), 8)
        span_up = pl.ds(pl.multiple_of(block * 8 + 8, 8), 8)
        now = [ref[span, :] for ref in fields]
        down = [
            jnp.where(sub_wide == 0, pltpu.roll(ref[span_down, :], 1, 0), pltpu.roll(value, 1, 0))
            for ref, value in zip(fields, now)
        ]
        up = [
            jnp.where(sub_wide == 7, pltpu.roll(ref[span_up, :], 7, 0), pltpu.roll(value, 7, 0))
            for ref, value in zip(fields, now)
        ]
        west = [pltpu.roll(value, 1, 1) for value in now]
        east = [pltpu.roll(value, width - 1, 1) for value in now]
        for ref, value in zip(fresh, gas_update(now, down, up, west, east)):
            ref[span, :] = value
        return _

    lax.fori_loop(1, blocks - 1, inner_rows, 0)

    column = lax.broadcasted_iota(jnp.int32, (padded, LANES), 1)
    row = lax.broadcasted_iota(jnp.int32, (padded, LANES), 0)
    group = lax.div(me * lines, height)
    index = lax.rem(me * lines, height) + row
    half = height // 2
    at_zero = jnp.where(index < half, gy * index, gy // 2 + gy * (index - half))
    m = jnp.where(group == 0, at_zero, group + gy * index)
    m = jnp.where(row == lines, ny // 2, jnp.where(row > lines, 1, m))
    shift = shift_ref[0]
    sigma = modulo(m * shift, ny)
    column = jnp.where(column < wide, column, column - wide)
    unit = 2.0 * jnp.pi / (nx * ny)
    points = (column * wide, column)
    for turns, point in zip((outer_turn, inner_turn), points):
        angle = modulo(sigma * point, nx * ny).astype(jnp.float32) * unit
        turns[0] = jnp.cos(angle)
        turns[1] = jnp.sin(angle)
    shear = sigma.astype(jnp.float32) / ny
    signed = jnp.where(m < ny // 2, m, m - ny).astype(jnp.float32)
    wave_y = 2.0 * jnp.pi / ny * signed
    wave_y = wave_y * wave_y
    weight = jnp.where(jnp.logical_or(m == 0, m == ny // 2), 1.0, 2.0) / (nx * ny)

    def fill(n, _):
        x_wave = n + outer * column
        x_signed = jnp.where(x_wave < nx // 2, x_wave, x_wave - nx).astype(jnp.float32)
        wave_x = 2.0 * jnp.pi / nx * (x_signed + shear)
        magnitude = jnp.sqrt(wave_x * wave_x + wave_y)
        anchor = jnp.logical_and(m == 0, x_wave == 0)
        safe = jnp.where(anchor, 1.0, magnitude)
        green[n] = jnp.where(anchor, 0.0, -jnp.exp(-thickness * safe) / safe) * weight
        return _

    for side in range(2):
        row_copy(side).wait_recv()
        col_each(side, incoming[side], arrive)
    here = azimuth * height

    def slid(side, amount, wraps):
        line = jnp.concatenate([cols[side, a] for a in range(gy)], axis=1)
        line = pltpu.roll(line, amount, 1)[:, :height]
        return jnp.where(wraps, line, cols[side, azimuth])

    ghost = jnp.concatenate(
        [
            slid(0, lax.rem(2 * ny - here - shift, ny), inner_edge),
            slid(1, lax.rem(ny - here + shift, ny), outer_edge),
        ],
        axis=0,
    ).T
    colbuf2[...] = ghost
    for block in (0, blocks - 1):
        at = block * 8
        now = [ref[at : at + 8, :] for ref in fields]
        sides = ghost[at : at + 8]
        down, up, west, east = [], [], [], []
        for f in range(3):
            edge = fields[f][at - 1 : at, :] if block else rows[0, f : f + 1, :]
            down.append(jnp.where(sub_wide == 0, edge, pltpu.roll(now[f], 1, 0)))
            edge = fields[f][at + 8 : at + 9, :] if block == 0 else rows[1, f : f + 1, :]
            up.append(jnp.where(sub_wide == 7, edge, pltpu.roll(now[f], 7, 0)))
            west.append(jnp.where(lane_wide == 0, sides[:, f : f + 1], pltpu.roll(now[f], 1, 1)))
            edge = pltpu.roll(now[f], width - 1, 1)
            east.append(jnp.where(lane_wide == width - 1, sides[:, 8 + f : 9 + f], edge))
        for ref, value in zip(fresh, gas_update(now, down, up, west, east)):
            ref[at : at + 8, :] = value
    sub2 = lax.broadcasted_iota(jnp.int32, (8, 2 * LANES), 0)
    lane2 = lax.broadcasted_iota(jnp.int32, (8, 2 * LANES), 1)

    def side_cells(block, _):
        span = pl.ds(pl.multiple_of(block * 8, 8), 8)
        span_down = pl.ds(pl.multiple_of(block * 8 - 8, 8), 8)
        span_up = pl.ds(pl.multiple_of(block * 8 + 8, 8), 8)
        sides = colbuf2[span, :]
        for end in range(2):
            start_lane = 0 if end == 0 else width - 2 * LANES
            window = slice(start_lane, start_lane + 2 * LANES)
            now, down, up, west, east = [], [], [], [], []
            for f, ref in enumerate(fields):
                value = ref[span, window]
                now.append(value)
                edge = pltpu.roll(ref[span_down, window], 1, 0)
                down.append(jnp.where(sub2 == 0, edge, pltpu.roll(value, 1, 0)))
                edge = pltpu.roll(ref[span_up, window], 7, 0)
                up.append(jnp.where(sub2 == 7, edge, pltpu.roll(value, 7, 0)))
                left = pltpu.roll(value, 1, 1)
                right = pltpu.roll(value, 2 * LANES - 1, 1)
                if end == 0:
                    left = jnp.where(lane2 == 0, sides[:, f : f + 1], left)
                else:
                    right = jnp.where(lane2 == 2 * LANES - 1, sides[:, 8 + f : 9 + f], right)
                west.append(left)
                east.append(right)
            target = slice(0, LANES) if end == 0 else slice(width - LANES, width)
            kept = slice(0, LANES) if end == 0 else slice(LANES, 2 * LANES)
            for ref, value in zip(fresh, gas_update(now, down, up, west, east)):
                ref[span, target] = value[:, kept]
        return _

    lax.fori_loop(1, blocks - 1, side_cells, 0)

    finals = [
        pltpu.make_async_copy(ref, final, field_sem.at[f])
        for f, (ref, final) in enumerate(zip(fresh, (d_final, x_final, y_final)))
    ]

    for part in range(4):
        for at in range(part * step1, (part + 1) * step1, 8):
            for tile in range(width // LANES):
                span = slice(tile * LANES, (tile + 1) * LANES)
                near = d_out[at : at + 8, span]
                far = d_out[at + packed : at + packed + 8, span]
                src[2 * tile, at : at + 8, :] = jnp.where(low, near, flip(far))
                src[2 * tile + 1, at : at + 8, :] = jnp.where(low, flip(near), far)
        each(functools.partial(one, part), gy, start)
    for final in finals:
        final.start()
    got1[azimuth] = src[azimuth]
    lax.fori_loop(0, outer, fill, 0)
    table_load.wait()

    for part in range(4):
        each(functools.partial(one, part), gy, arrive)
        for at in range(part * step1, (part + 1) * step1, 8):
            f = [got1[a, at : at + 8, :] for a in range(gy)]
            plus = [None] + [f[a] + f[gy - a] for a in range(1, half_gy)]
            minus = [None] + [f[a] - f[gy - a] for a in range(1, half_gy)]

            def put(group, base, value):
                stage[group, base + at : base + at + 8, :] = value
                stage[group, base + packed + at : base + packed + at + 8, :] = flip(value)

            for g in range(half_gy + 1):
                re = f[0] + f[half_gy] if g % 2 == 0 else f[0] - f[half_gy]
                im = None
                for a in range(1, half_gy):
                    angle = 2.0 * np.pi * ((a * g) % gy) / gy
                    re = re + float(np.cos(angle)) * plus[a]
                    if 0 < g < half_gy:
                        term = float(-np.sin(angle)) * minus[a]
                        im = term if im is None else im + term
                if g == half_gy:
                    put(0, height, re)
                else:
                    put(g, 0, re)
                    if g:
                        put(g, height, im)
    lane = lax.broadcasted_iota(jnp.int32, (height, LANES), 1)
    ratio = height // lines
    for g in range(half_gy):
        both = dot3((y_table[0, g], y_table[1, g]), split(stage[g]), ((1,), (0,)))
        value = jnp.where(lane < wide, both[:height], flip(both[height:]))
        for q in range(ratio):
            give2[g * ratio + q] = value[q * lines : (q + 1) * lines]
    for part in range(parts2):
        each(functools.partial(two, part), count, start)
    got2[me] = give2[me]

    def turned(value, c, s):
        return value * c + flip(value) * s

    def solve(load, rows, store):
        ci, si = inner_turn[0, rows, :], inner_turn[1, rows, :] * signs
        co, so = outer_turn[0, rows, :], outer_turn[1, rows, :]
        parts = [turned(load(d), co[:, d : d + 1], -so[:, d : d + 1] * signs) for d in range(outer)]
        parts = fft_packed(parts, -1.0, signs)
        for n in range(outer):
            value = turned(parts[n], ci, -si)
            mid[n] = turned(value, turn[0, n : n + 1, :], turn[1, n : n + 1, :])
        modes = dot3(split(mid[...].reshape(outer * 8, LANES)), (x_table[0], x_table[1]), ((1,), (0,)))
        modes = modes * green[:, rows, :].reshape(outer * 8, LANES)
        modes = dot3(split(modes), (x_table[0], x_table[1]), ((1,), (1,)))
        mid[...] = modes.reshape(outer, 8, LANES)
        parts = []
        for n in range(outer):
            value = turned(mid[n], turn[0, n : n + 1, :], -turn[1, n : n + 1, :])
            parts.append(turned(value, ci, si))
        parts = fft_packed(parts, 1.0, signs)
        for d in range(outer):
            store(d, turned(parts[d], co[:, d : d + 1], so[:, d : d + 1] * signs))

    def load_extra(d):
        return jnp.where(jnp.logical_and(sub8 == 0, low), flip(got2[d, 0:8, :]), 0.0)

    def store_extra(d, value):
        extra[d] = flip(value)

    def chunk(part, _):
        each(functools.partial(two, part), count, arrive)
        rows = pl.ds(pl.multiple_of(part * 8, 8), 8)

        @pl.when(jnp.logical_and(part == 0, first))
        def _extra():
            solve(load_extra, pl.ds(lines, 8), store_extra)

        corner = jnp.logical_and(jnp.logical_and(sub8 == 0, lane8 >= wide), part == 0)
        damp = jnp.where(corner, keep, 1.0)
        mine = jnp.logical_and(corner, first)

        def load(d):
            return got2[d, rows, :] * damp

        def store(d, value):
            give3[d, rows, :] = jnp.where(mine, extra[d], value)

        solve(load, rows, store)
        each(functools.partial(three, part), count, start)
        return _

    lax.fori_loop(0, parts2, chunk, 0)
    got3[me] = give3[me]
    for part in range(parts2):
        each(functools.partial(three, part), count, arrive)

    for g in range(half_gy):
        value = got3[g * ratio : (g + 1) * ratio].reshape(height, LANES)
        value = jnp.concatenate([value, flip(value)], axis=0)
        stage[g] = dot3((y_table[0, g], y_table[1, g]), split(value), ((0,), (0,)))

    def take(group, base, at):
        near = stage[group, base + at : base + at + 8, :]
        far = stage[group, base + packed + at : base + packed + at + 8, :]
        return jnp.where(low, near, flip(far))

    for part in range(4):
        for at in range(part * step1, (part + 1) * step1, 8):
            re = [take(g, 0, at) for g in range(half_gy)]
            im = [None] + [take(g, height, at) for g in range(1, half_gy)]
            last = take(0, height, at)
            for a in range(half_gy + 1):
                even = re[0] + last if a % 2 == 0 else re[0] - last
                odd = None
                for g in range(1, half_gy):
                    angle = 2.0 * np.pi * ((a * g) % gy) / gy
                    even = even + float(np.cos(angle)) * re[g]
                    if 0 < a < half_gy:
                        term = float(np.sin(angle)) * im[g]
                        odd = term if odd is None else odd + term
                if odd is None:
                    give4[a, at : at + 8, :] = even
                else:
                    give4[a, at : at + 8, :] = even - odd
                    give4[gy - a, at : at + 8, :] = even + odd
        each(functools.partial(four, part), gy, start)
    out[azimuth] = give4[azimuth]
    for final in finals:
        final.wait()
    for side in range(2):
        row_copy(side).wait_send()
        col_each(side, outgoing[side], leave)
    for part in range(4):
        each(functools.partial(one, part), gy, leave)
    for part in range(parts2):
        each(functools.partial(two, part), count, leave)
        each(functools.partial(three, part), count, leave)
    for part in range(4):
        each(functools.partial(four, part), gy, arrive)
        each(functools.partial(four, part), gy, leave)


def fused_step(shift, fields, tables, nx, ny, gx, gy, ident):
    height, width = fields[0].shape
    packed = height // 2
    count = gx * gy
    lines = ny // 2 // count
    padded = lines + 8
    f32 = jnp.float32
    blocks = (gy, packed, LANES)
    sems = [pltpu.SemaphoreType.DMA((2, gy))] * 2 + [pltpu.SemaphoreType.DMA((2,))] * 2
    for parts, peers in ((4, gy), (lines // 8, count), (lines // 8, count), (4, gy)):
        sems += [pltpu.SemaphoreType.DMA((parts, peers))] * 2
    shape = jax.ShapeDtypeStruct((height, width), f32)
    return pl.pallas_call(
        functools.partial(fused_kernel, nx, ny),
        out_shape=(shape, shape, shape, jax.ShapeDtypeStruct(blocks, f32)),
        in_specs=[pl.BlockSpec(memory_space=pltpu.SMEM)]
        + [VMEM] * 3
        + [pl.BlockSpec(memory_space=pl.ANY)]
        + [VMEM] * (len(tables) - 1),
        out_specs=(pl.BlockSpec(memory_space=pl.ANY),) * 3 + (VMEM,),
        scratch_shapes=[pltpu.VMEM((height, width), f32)] * 3
        + [
            pltpu.VMEM(tables[0].shape, tables[0].dtype),
            pltpu.SemaphoreType.DMA,
            pltpu.SemaphoreType.DMA((3,)),
            pltpu.VMEM((2, gy, 8, height), f32),
            pltpu.VMEM((2, 8, width), f32),
            pltpu.VMEM((2, 8, height), f32),
            pltpu.VMEM((height, 16), f32),
            pltpu.VMEM((2, 8, width), f32),
            pltpu.VMEM((2, padded, LANES), f32),
            pltpu.VMEM((2, padded, LANES), f32),
            pltpu.VMEM(blocks, f32),
            pltpu.VMEM(blocks, f32),
            pltpu.VMEM((gy // 2, 2 * height, LANES), f32),
            pltpu.VMEM((count, lines, LANES), f32),
            pltpu.VMEM((count, lines, LANES), f32),
            pltpu.VMEM((count, padded, LANES), f32),
            pltpu.VMEM((count, 8, LANES), f32),
            pltpu.VMEM((count, 8, LANES), f32),
            pltpu.VMEM((count, lines, LANES), f32),
            pltpu.VMEM((count, lines, LANES), f32),
            pltpu.VMEM(blocks, f32),
        ]
        + sems,
        compiler_params=pltpu.CompilerParams(collective_id=ident, has_side_effects=True),
    )(shift, *fields, *tables)


def shards(density, xmomentum, ymomentum, shear_shift):
    gx, gy = lax.axis_size("gx"), lax.axis_size("gy")
    here_x, here_y = lax.axis_index("gx"), lax.axis_index("gy")
    height, width = density.shape[1:]
    nx, ny = width * gx, height * gy
    count = gx * gy
    xb = width // gy
    lines = ny // 2 // count
    shift = shear_shift[0]
    fields = [density[0], xmomentum[0], ymomentum[0]]

    fold = LANES // xb
    packed = height // fold
    wide = LANES // 2
    outer = nx // wide
    group = wide // xb
    y_table = jnp.asarray(azimuth_table(gy, height))
    turn, table = radial_tables(nx)
    turn, table = jnp.asarray(turn), jnp.asarray(table)
    if group == 1 and packed % 32 == 0 and lines % 8 == 0 and height % lines == 0:
        results = fused_step(shear_shift, fields, (y_table, turn, table), nx, ny, gx, gy, 1)
        return tuple(r[None] for r in unpack(results[:3], results[3]))

    cols, rows = halo(fields, gx, gy, 0)
    cols = jnp.transpose(cols, (0, 2, 1, 3)).reshape(2, 8, ny)
    cols = jnp.concatenate([cols, cols], axis=2)
    start_left = (here_y * height + jnp.where(here_x == 0, shift, 0)) % ny
    start_right = (here_y * height - jnp.where(here_x == gx - 1, shift, 0)) % ny
    ghost = jnp.stack(
        [
            lax.dynamic_slice_in_dim(cols[0], start_left, height, 1),
            lax.dynamic_slice_in_dim(cols[1], start_right, height, 1),
        ]
    )
    density_new, xmomentum_new, ymomentum_new = gas(fields, rows, ghost)
    padded = (lines + 8) // 8 * 8
    row = jnp.arange(padded, dtype=jnp.int32)
    slot = (here_x * gy + here_y) * lines + row
    wave = slot_wave(slot // height, slot % height, gy, height)
    wave = jnp.where(row == lines, ny // 2, jnp.where(row > lines, 1, wave))
    sigma = wave * shift % ny
    unit = 2.0 * jnp.pi / (nx * ny)

    def phases(points):
        angle = (sigma[:, None] * points[None, :] % (nx * ny)).astype(jnp.float32) * unit
        return jnp.stack([jnp.cos(angle), jnp.sin(angle)])

    lane = jnp.arange(LANES, dtype=jnp.int32)
    outer_turn = phases(jnp.where(lane < outer, lane, 0) * wide)
    inner_turn = phases(lane % wide)
    full = (padded, LANES)
    line_tables = (
        jnp.broadcast_to(wave[:, None], full),
        jnp.broadcast_to(sigma[:, None], full),
        outer_turn,
        inner_turn,
        turn,
        table,
    )

    blocks = jnp.transpose(density_new.reshape(fold, packed, gy, xb), (2, 1, 0, 3))
    blocks = exchange(blocks.reshape(gy, packed, LANES), gy, False, 1)
    slots = azimuth_forward(blocks, y_table, xb)
    slots = slots[:, :, : 2 * xb].reshape(count, lines, 2 * xb)
    slots = exchange(slots, gy, True, 2)
    if group > 1:
        slots = slots.reshape(outer, group, lines, 2, xb)
        slots = jnp.transpose(slots, (0, 2, 3, 1, 4)).reshape(outer, lines, LANES)
    solved = radial(slots, *line_tables, nx, ny)
    if group > 1:
        solved = solved.reshape(outer, lines, 2, group, xb)
        solved = jnp.transpose(solved, (0, 3, 1, 2, 4)).reshape(count, lines, 2 * xb)
    solved = exchange(solved, gy, True, 3).reshape(gy // 2, height, 2 * xb)
    solved = jnp.pad(solved, ((0, 0), (0, 0), (0, LANES - 2 * xb)))
    lined = azimuth_back(solved, y_table, xb, gy, packed)
    lined = exchange(lined, gy, False, 4)
    potential = jnp.transpose(lined.reshape(gy, packed, fold, xb), (2, 1, 0, 3))
    potential = potential.reshape(height, width)
    return (density_new[None], xmomentum_new[None], ymomentum_new[None], potential[None])


def solution(mesh):
    split_spec = P(None, "gy", "gx")
    return jax.shard_map(
        shards,
        mesh=mesh,
        in_specs=(split_spec, split_spec, split_spec, P()),
        out_specs=(split_spec,) * 4,
        check_vma=False,
    )
```

profile of v0, /device:TPU:0, one launch (start us, length us, event | category | flops | bytes accessed | tf_op | source)
XLA Modules:
  0.0 82.3 jit_solution(11590171141761568457)
XLA Ops:
  1.3 78.0 %shard_map.102 = (f32[128,1024]{1,0:T(8,128)}, f32[128,1024]{1,0:T(8,128)}, f32[128,1024]{1,0:T(8,128)}, f32[16,64,128]{2,1,0:T(8,128)}) custom-call(s32[1]{0:T(128)S(6)} %copy.11.shift_ref, f32[128,1024]{1,0:T(8,128)} %bitcast.7, f32[128,1024]{1,0:T(8,128)} %bitcast.8, f32[128,1024]{1,0:T(8,128)} %bitcast.9, ...), custom_call_target="tpu_custom_call" | custom-call | tf_op jit(solution)/shard_map/pallas_call | solution.py:993
  79.3 3.0 %shard_map.103 = (f32[128,1024]{1,0:T(8,128)}, f32[128,1024]{1,0:T(8,128)}, f32[128,1024]{1,0:T(8,128)}, f32[128,1024]{1,0:T(8,128)}) custom-call(f32[128,1024]{1,0:T(8,128)} %get-tuple-element.12.d_ref, f32[128,1024]{1,0:T(8,128)} %get-tuple-element.13.x_ref, f32[128,1024]{1,0:T(8,128)} %get-tuple-element.14.y_ref, f32[16,64,128]{2,1,0:T(8,128)} %get-tuple-element.15.src), custom_call_target="tpu_custom_call" | custom-call | tf_op jit(solution)/shard_map/pallas_call | solution.py:274
where the time goes:
time: 82.5 us; the launch traced here: 82.3 us
  Pallas kernels  81 us (98%)
  between operations  1.29 us (2%)
    pallas_call x1, Pallas kernels, fused_step(): pl.pallas_call(functools.partial(fused_kernel, nx, ny), out_shape=(shape,...  78 us
    pallas_call x1, Pallas kernels, unpack(): pl.pallas_call(unpack_kernel, out_shape=(shape,) * 4, in_specs=[VMEM] * 4...  3 us

commit v1 on v0

--- a/solution.py
+++ b/solution.py
@@ -627,21 +627,29 @@
         return pltpu.make_async_remote_copy(
             src_ref=colbuf.at[side],
             dst_ref=cols.at[1 - side, azimuth],
-            send_sem=csend.at[side, k],
-            recv_sem=crecv.at[side, k],
+            send_sem=csend.at[side],
+            recv_sem=crecv.at[side],
             device_id=(before if side == 0 else after, lax.rem(azimuth + k, gy)),
             device_id_type=MESH,
         )
 
     outgoing = (jnp.where(inner_edge, gy, 1), jnp.where(outer_edge, gy, 1))
-    incoming = (jnp.where(outer_edge, gy, 1), jnp.where(inner_edge, gy, 1))
-
-    def col_each(side, peers, act):
+
+    def col_start(side):
         def body(k, _):
-            act(col_copy(side, k))
+            col_copy(side, k).start()
             return _
 
-        lax.fori_loop(0, peers, body, 0)
+        lax.fori_loop(0, outgoing[side], body, 0)
+
+    def col_wait(side, many, sem):
+        @pl.when(many)
+        def _all():
+            pltpu.make_async_copy(cols.at[side], cols.at[side], sem.at[side]).wait()
+
+        @pl.when(jnp.logical_not(many))
+        def _one():
+            pltpu.make_async_copy(cols.at[side, 0], cols.at[side, 0], sem.at[side]).wait()
 
     def line_copy(give, got, send, recv, rows, part, k):
         peer = lax.rem(azimuth + k, gy)
@@ -649,8 +657,8 @@
         return pltpu.make_async_remote_copy(
             src_ref=give.at[peer, span],
             dst_ref=got.at[azimuth, span],
-            send_sem=send.at[part, k],
-            recv_sem=recv.at[part, k],
+            send_sem=send,
+            recv_sem=recv.at[part],
             device_id=(radial_at, peer),
             device_id_type=MESH,
         )
@@ -661,27 +669,28 @@
         return pltpu.make_async_remote_copy(
             src_ref=give.at[peer, span],
             dst_ref=got.at[me, span],
-            send_sem=send.at[part, k],
-            recv_sem=recv.at[part, k],
+            send_sem=send,
+            recv_sem=recv.at[part],
             device_id=device_of(peer),
             device_id_type=MESH,
         )
 
-    def each(copy, peers, act):
+    def each(copy, peers):
         def body(k, _):
-            act(copy(k))
+            copy(k).start()
             return _
 
-        lax.fori_loop(1, peers, body, 0)
-
-    def start(c):
-        c.start()
-
-    def arrive(c):
-        c.wait_recv()
-
-    def leave(c):
-        c.wait_send()
+        lax.fori_loop(peers // 2, peers, body, 0)
+        lax.fori_loop(1, peers // 2, body, 0)
+
+    def arrive(got, recv, rows, part):
+        span = pl.ds(pl.multiple_of(part * rows, rows), rows)
+        whole = got.at[pl.ds(0, got.shape[0] - 1), span]
+        pltpu.make_async_copy(whole, whole, recv.at[part]).wait()
+
+    def leave(give, send):
+        whole = give.at[pl.ds(0, give.shape[0] - 1)]
+        pltpu.make_async_copy(whole, whole, send).wait()
 
     one = functools.partial(line_copy, src, got1, send1, recv1, step1)
     two = functools.partial(all_copy, give2, got2, send2, recv2, 8)
@@ -691,7 +700,7 @@
     pl.semaphore_wait(barrier, count - 1)
     for side in range(2):
         row_copy(side).start()
-        col_each(side, outgoing[side], start)
+        col_start(side)
 
     blocks = height // 8
     sub_wide = lax.broadcasted_iota(jnp.int32, (8, width), 0)
@@ -753,7 +762,7 @@
 
     for side in range(2):
         row_copy(side).wait_recv()
-        col_each(side, incoming[side], arrive)
+        col_wait(side, outer_edge if side == 0 else inner_edge, crecv)
     here = azimuth * height
 
     def slid(side, amount, wraps):
@@ -832,7 +841,7 @@
                 far = d_out[at + packed : at + packed + 8, span]
                 src[2 * tile, at : at + 8, :] = jnp.where(low, near, flip(far))
                 src[2 * tile + 1, at : at + 8, :] = jnp.where(low, flip(near), far)
-        each(functools.partial(one, part), gy, start)
+        each(functools.partial(one, part), gy)
     for final in finals:
         final.start()
     got1[azimuth] = src[azimuth]
@@ -840,7 +849,7 @@
     table_load.wait()
 
     for part in range(4):
-        each(functools.partial(one, part), gy, arrive)
+        arrive(got1, recv1, step1, part)
         for at in range(part * step1, (part + 1) * step1, 8):
             f = [got1[a, at : at + 8, :] for a in range(gy)]
             plus = [None] + [f[a] + f[gy - a] for a in range(1, half_gy)]
@@ -873,7 +882,7 @@
         for q in range(ratio):
             give2[g * ratio + q] = value[q * lines : (q + 1) * lines]
     for part in range(parts2):
-        each(functools.partial(two, part), count, start)
+        each(functools.partial(two, part), count)
     got2[me] = give2[me]
 
     def turned(value, c, s):
@@ -906,7 +915,7 @@
         extra[d] = flip(value)
 
     def chunk(part, _):
-        each(functools.partial(two, part), count, arrive)
+        arrive(got2, recv2, 8, part)
         rows = pl.ds(pl.multiple_of(part * 8, 8), 8)
 
         @pl.when(jnp.logical_and(part == 0, first))
@@ -924,13 +933,13 @@
             give3[d, rows, :] = jnp.where(mine, extra[d], value)
 
         solve(load, rows, store)
-        each(functools.partial(three, part), count, start)
+        each(functools.partial(three, part), count)
         return _
 
     lax.fori_loop(0, parts2, chunk, 0)
     got3[me] = give3[me]
     for part in range(parts2):
-        each(functools.partial(three, part), count, arrive)
+        arrive(got3, recv3, 8, part)
 
     for g in range(half_gy):
         value = got3[g * ratio : (g + 1) * ratio].reshape(height, LANES)
@@ -961,21 +970,19 @@
                 else:
                     give4[a, at : at + 8, :] = even - odd
                     give4[gy - a, at : at + 8, :] = even + odd
-        each(functools.partial(four, part), gy, start)
+        each(functools.partial(four, part), gy)
     out[azimuth] = give4[azimuth]
     for final in finals:
         final.wait()
     for side in range(2):
         row_copy(side).wait_send()
-        col_each(side, outgoing[side], leave)
+        col_wait(side, inner_edge if side == 0 else outer_edge, csend)
+    leave(src, send1)
+    leave(give2, send2)
+    leave(give3, send3)
     for part in range(4):
-        each(functools.partial(one, part), gy, leave)
-    for part in range(parts2):
-        each(functools.partial(two, part), count, leave)
-        each(functools.partial(three, part), count, leave)
-    for part in range(4):
-        each(functools.partial(four, part), gy, arrive)
-        each(functools.partial(four, part), gy, leave)
+        arrive(out, recv4, step1, part)
+    leave(give4, send4)
 
 
 def fused_step(shift, fields, tables, nx, ny, gx, gy, ident):
@@ -986,9 +993,9 @@
     padded = lines + 8
     f32 = jnp.float32
     blocks = (gy, packed, LANES)
-    sems = [pltpu.SemaphoreType.DMA((2, gy))] * 2 + [pltpu.SemaphoreType.DMA((2,))] * 2
-    for parts, peers in ((4, gy), (lines // 8, count), (lines // 8, count), (4, gy)):
-        sems += [pltpu.SemaphoreType.DMA((parts, peers))] * 2
+    sems = [pltpu.SemaphoreType.DMA((2,))] * 4
+    for parts in (4, lines // 8, lines // 8, 4):
+        sems += [pltpu.SemaphoreType.DMA, pltpu.SemaphoreType.DMA((parts,))]
     shape = jax.ShapeDtypeStruct((height, width), f32)
     return pl.pallas_call(
         functools.partial(fused_kernel, nx, ny),

time: 82.5 us -> 75 us (0.909)
  Pallas kernels: 81 us -> 73.6 us
    pallas_call x1, Pallas kernels: 78 us -> 70.6 us  [fused_step(): pl.pallas_call(functools.partial(fused_kernel, nx, ny), out_shape=(shape,...]
where the time goes in v1:
time: 75 us; the launch traced here: 74.9 us
  Pallas kernels  73.6 us (98%)
  between operations  1.29 us (2%)
    pallas_call x1, Pallas kernels, fused_step(): pl.pallas_call(functools.partial(fused_kernel, nx, ny), out_shape=(shape,...  70.6 us
    pallas_call x1, Pallas kernels, unpack(): pl.pallas_call(unpack_kernel, out_shape=(shape,) * 4, in_specs=[VMEM] * 4...  3 us

profile of v1, /device:TPU:0, one launch (start us, length us, event | category | flops | bytes accessed | tf_op | source)
XLA Modules:
  0.0 74.9 jit_solution(17672562840908021737)
XLA Ops:
  1.3 70.6 %shard_map.102 = (f32[128,1024]{1,0:T(8,128)}, f32[128,1024]{1,0:T(8,128)}, f32[128,1024]{1,0:T(8,128)}, f32[16,64,128]{2,1,0:T(8,128)}) custom-call(s32[1]{0:T(128)S(6)} %copy.11.shift_ref, f32[128,1024]{1,0:T(8,128)} %bitcast.7, f32[128,1024]{1,0:T(8,128)} %bitcast.8, f32[128,1024]{1,0:T(8,128)} %bitcast.9, ...), custom_call_target="tpu_custom_call" | custom-call | tf_op jit(solution)/shard_map/pallas_call | solution.py:1000
  71.9 3.0 %shard_map.103 = (f32[128,1024]{1,0:T(8,128)}, f32[128,1024]{1,0:T(8,128)}, f32[128,1024]{1,0:T(8,128)}, f32[128,1024]{1,0:T(8,128)}) custom-call(f32[128,1024]{1,0:T(8,128)} %get-tuple-element.12.d_ref, f32[128,1024]{1,0:T(8,128)} %get-tuple-element.13.x_ref, f32[128,1024]{1,0:T(8,128)} %get-tuple-element.14.y_ref, f32[16,64,128]{2,1,0:T(8,128)} %get-tuple-element.15.src), custom_call_target="tpu_custom_call" | custom-call | tf_op jit(solution)/shard_map/pallas_call | solution.py:274

commit v2 on v1

--- a/solution.py
+++ b/solution.py
@@ -18,6 +18,7 @@
 LANES = 128
 MESH = pl.DeviceIdType.MESH
 VMEM = pl.BlockSpec(memory_space=pltpu.VMEM)
+HBM = pl.BlockSpec(memory_space=pl.ANY)
 
 
 def split_np(table):
@@ -200,6 +201,11 @@
         0.5 * (fl + fr) - 0.5 * speed * (r - l)
         for l, r, fl, fr in zip(left, right, left_flux, right_flux)
     ]
+
+
+def mass_flux(low, high, low_momentum, high_momentum, low_speed, high_speed):
+    speed = jnp.maximum(low_speed, high_speed) + sound_speed
+    return 0.5 * (low_momentum + high_momentum) - 0.5 * speed * (high - low)
 
 
 def gas_update(now, down, up, west, east):
@@ -256,17 +262,29 @@
     )(*fields, rows, cols)
 
 
-def unpack_kernel(d_ref, x_ref, y_ref, src, d_out, x_out, y_out, out):
-    d_out[...] = d_ref[...]
-    x_out[...] = x_ref[...]
-    y_out[...] = y_ref[...]
+def unpack_kernel(d_in, x_in, y_in, src_in, d_out, x_out, y_out, out, d, x, y, src, packed_out, get, put):
     gy, packed, _ = src.shape
     low = lax.broadcasted_iota(jnp.int32, (packed, LANES), 1) < LANES // 2
+    sources, buffers, targets = (src_in, d_in, x_in, y_in), (src, d, x, y), (out, d_out, x_out, y_out)
+    gets = [pltpu.make_async_copy(a, b, get.at[f]) for f, (a, b) in enumerate(zip(sources, buffers))]
+    puts = [
+        pltpu.make_async_copy(a, b, put.at[f])
+        for f, (a, b) in enumerate(zip((packed_out,) + buffers[1:], targets))
+    ]
+    for copy in gets:
+        copy.start()
+    gets[0].wait()
     for tile in range(gy // 2):
         span = slice(tile * LANES, (tile + 1) * LANES)
         near, far = src[2 * tile], src[2 * tile + 1]
-        out[0:packed, span] = jnp.where(low, near, flip(far))
-        out[packed : 2 * packed, span] = jnp.where(low, flip(near), far)
+        packed_out[0:packed, span] = jnp.where(low, near, flip(far))
+        packed_out[packed : 2 * packed, span] = jnp.where(low, flip(near), far)
+    puts[0].start()
+    for f in range(1, 4):
+        gets[f].wait()
+        puts[f].start()
+    for copy in puts:
+        copy.wait()
 
 
 def unpack(fields, blocks):
@@ -274,8 +292,11 @@
     return pl.pallas_call(
         unpack_kernel,
         out_shape=(shape,) * 4,
-        in_specs=[VMEM] * 4,
-        out_specs=(VMEM,) * 4,
+        in_specs=[HBM] * 4,
+        out_specs=(HBM,) * 4,
+        scratch_shapes=[pltpu.VMEM(fields[0].shape, jnp.float32)] * 3
+        + [pltpu.VMEM(blocks.shape, jnp.float32), pltpu.VMEM(fields[0].shape, jnp.float32)]
+        + [pltpu.SemaphoreType.DMA((4,))] * 2,
     )(*fields, blocks)
 
 
@@ -557,8 +578,9 @@
 
 
 def fused_kernel(
-    nx, ny, shift_ref, d_ref, x_ref, y_ref, y_source, turn, x_table, d_final, x_final, y_final, out,
-    d_out, x_out, y_out, y_table, table_sem, field_sem,
+    nx, ny, shift_in, d_in, x_in, y_in, y_table_in, turn_in, x_table_in, d_final, x_final, y_final, out,
+    shift_ref, d_ref, x_ref, y_ref, d_out, x_out, y_out, y_table, turn, x_table,
+    shift_sem, load_sem, table_sem, field_sem, own_sem,
     cols, rows, colbuf, colbuf2, rowbuf, outer_turn, inner_turn, src,
     got1, stage, give2, got2, green, mid, extra, give3, got3, give4,
     csend, crecv, rsend, rrecv, send1, recv1, send2, recv2, send3, recv3, send4, recv4,
@@ -593,8 +615,15 @@
     def device_of(peer):
         return lax.div(peer, gy), lax.rem(peer, gy)
 
-    table_load = pltpu.make_async_copy(y_source, y_table, table_sem)
-    table_load.start()
+    loads = [
+        pltpu.make_async_copy(source, ref, load_sem.at[f])
+        for f, (source, ref) in enumerate(zip((d_in, x_in, y_in), fields))
+    ]
+    shift_load = pltpu.make_async_copy(shift_in, shift_ref, shift_sem)
+    table_loads = [
+        pltpu.make_async_copy(source, ref, table_sem.at[f])
+        for f, (source, ref) in enumerate(zip((y_table_in, turn_in, x_table_in), (y_table, turn, x_table)))
+    ]
     cols[...] = jnp.zeros_like(cols)
     barrier = pltpu.get_barrier_semaphore()
 
@@ -603,10 +632,17 @@
         pl.semaphore_signal(barrier, inc=1, device_id=there, device_id_type=MESH)
         return _
 
+    for load in loads:
+        load.start()
+    shift_load.start()
     lax.fori_loop(1, count, greet, 0)
+    for load in table_loads:
+        load.start()
 
     rowbuf[...] = jnp.zeros_like(rowbuf)
     colbuf[...] = jnp.zeros_like(colbuf)
+    for load in loads:
+        load.wait()
     for at, ref in enumerate(fields):
         rowbuf[0, at : at + 1, :] = ref[0:1, :]
         rowbuf[1, at : at + 1, :] = ref[height - 1 : height, :]
@@ -706,26 +742,40 @@
     sub_wide = lax.broadcasted_iota(jnp.int32, (8, width), 0)
     lane_wide = lax.broadcasted_iota(jnp.int32, (8, width), 1)
 
-    def inner_rows(block, _):
+    def density_rows(span, edge_down, edge_up):
+        now = [ref[span, :] for ref in fields]
+        rho, along, across = now
+        speed = jnp.abs(along / rho)
+        west = mass_flux(
+            pltpu.roll(rho, 1, 1), rho, pltpu.roll(along, 1, 1), along, pltpu.roll(speed, 1, 1), speed
+        )
+        west = jnp.where(lane_wide == 0, 0.0, west)
+        change = pltpu.roll(west, width - 1, 1) - west
+        down = [
+            jnp.where(sub_wide == 0, edge_down[f], pltpu.roll(now[f], 1, 0)) for f in (0, 2)
+        ]
+        up = [jnp.where(sub_wide == 7, edge_up[f], pltpu.roll(now[f], 7, 0)) for f in (0, 2)]
+        speed = jnp.abs(across / rho)
+        low_speed, high_speed = jnp.abs(down[1] / down[0]), jnp.abs(up[1] / up[0])
+        change = change + (
+            mass_flux(rho, up[0], across, up[1], speed, high_speed)
+            - mass_flux(down[0], rho, down[1], across, low_speed, speed)
+        )
+        d_out[span, :] = rho - time_step * change
+
+    def density_inner(block, _):
         span = pl.ds(pl.multiple_of(block * 8, 8), 8)
         span_down = pl.ds(pl.multiple_of(block * 8 - 8, 8), 8)
         span_up = pl.ds(pl.multiple_of(block * 8 + 8, 8), 8)
-        now = [ref[span, :] for ref in fields]
-        down = [
-            jnp.where(sub_wide == 0, pltpu.roll(ref[span_down, :], 1, 0), pltpu.roll(value, 1, 0))
-            for ref, value in zip(fields, now)
-        ]
-        up = [
-            jnp.where(sub_wide == 7, pltpu.roll(ref[span_up, :], 7, 0), pltpu.roll(value, 7, 0))
-            for ref, value in zip(fields, now)
-        ]
-        west = [pltpu.roll(value, 1, 1) for value in now]
-        east = [pltpu.roll(value, width - 1, 1) for value in now]
-        for ref, value in zip(fresh, gas_update(now, down, up, west, east)):
-            ref[span, :] = value
+        density_rows(
+            span,
+            [pltpu.roll(ref[span_down, :], 1, 0) for ref in fields],
+            [pltpu.roll(ref[span_up, :], 7, 0) for ref in fields],
+        )
         return _
 
-    lax.fori_loop(1, blocks - 1, inner_rows, 0)
+    lax.fori_loop(1, blocks - 1, density_inner, 0)
+    shift_load.wait()
 
     column = lax.broadcasted_iota(jnp.int32, (padded, LANES), 1)
     row = lax.broadcasted_iota(jnp.int32, (padded, LANES), 0)
@@ -780,8 +830,64 @@
     colbuf2[...] = ghost
     for block in (0, blocks - 1):
         at = block * 8
+        edge_down = [ref[at - 1 : at, :] if block else rows[0, f : f + 1, :] for f, ref in enumerate(fields)]
+        edge_up = [ref[at + 8 : at + 9, :] if block == 0 else rows[1, f : f + 1, :] for f, ref in enumerate(fields)]
+        density_rows(slice(at, at + 8), edge_down, edge_up)
+    lane_tile = lax.broadcasted_iota(jnp.int32, (height, LANES), 1)
+    for end in range(2):
+        span = slice(0, LANES) if end == 0 else slice(width - LANES, width)
+        mine = (d_ref[:, span], x_ref[:, span])
+        other = (ghost[:, 8 * end : 8 * end + 1], ghost[:, 8 * end + 1 : 8 * end + 2])
+        low_cell, high_cell = (other, mine) if end == 0 else (mine, other)
+        flux = mass_flux(
+            low_cell[0], high_cell[0], low_cell[1], high_cell[1],
+            jnp.abs(low_cell[1] / low_cell[0]), jnp.abs(high_cell[1] / high_cell[0]),
+        )
+        flux = jnp.where(lane_tile == (0 if end == 0 else LANES - 1), time_step * flux, 0.0)
+        d_out[:, span] = d_out[:, span] + flux if end == 0 else d_out[:, span] - flux
+
+    finals = [
+        pltpu.make_async_copy(ref, final, field_sem.at[f])
+        for f, (ref, final) in enumerate(zip(fresh, (d_final, x_final, y_final)))
+    ]
+
+    for part in range(4):
+        for at in range(part * step1, (part + 1) * step1, 8):
+            for tile in range(width // LANES):
+                span = slice(tile * LANES, (tile + 1) * LANES)
+                near = d_out[at : at + 8, span]
+                far = d_out[at + packed : at + packed + 8, span]
+                src[2 * tile, at : at + 8, :] = jnp.where(low, near, flip(far))
+                src[2 * tile + 1, at : at + 8, :] = jnp.where(low, flip(near), far)
+        each(functools.partial(one, part), gy)
+    finals[0].start()
+    got1[azimuth] = src[azimuth]
+
+    def inner_rows(block, _):
+        span = pl.ds(pl.multiple_of(block * 8, 8), 8)
+        span_down = pl.ds(pl.multiple_of(block * 8 - 8, 8), 8)
+        span_up = pl.ds(pl.multiple_of(block * 8 + 8, 8), 8)
+        now = [ref[span, :] for ref in fields]
+        down = [
+            jnp.where(sub_wide == 0, pltpu.roll(ref[span_down, :], 1, 0), pltpu.roll(value, 1, 0))
+            for ref, value in zip(fields, now)
+        ]
+        up = [
+            jnp.where(sub_wide == 7, pltpu.roll(ref[span_up, :], 7, 0), pltpu.roll(value, 7, 0))
+            for ref, value in zip(fields, now)
+        ]
+        west = [pltpu.roll(value, 1, 1) for value in now]
+        east = [pltpu.roll(value, width - 1, 1) for value in now]
+        for ref, value in zip(fresh[1:], gas_update(now, down, up, west, east)[1:]):
+            ref[span, :] = value
+        return _
+
+    lax.fori_loop(1, blocks - 1, inner_rows, 0)
+
+    for block in (0, blocks - 1):
+        at = block * 8
         now = [ref[at : at + 8, :] for ref in fields]
-        sides = ghost[at : at + 8]
+        sides = colbuf2[at : at + 8]
         down, up, west, east = [], [], [], []
         for f in range(3):
             edge = fields[f][at - 1 : at, :] if block else rows[0, f : f + 1, :]
@@ -791,7 +897,7 @@
             west.append(jnp.where(lane_wide == 0, sides[:, f : f + 1], pltpu.roll(now[f], 1, 1)))
             edge = pltpu.roll(now[f], width - 1, 1)
             east.append(jnp.where(lane_wide == width - 1, sides[:, 8 + f : 9 + f], edge))
-        for ref, value in zip(fresh, gas_update(now, down, up, west, east)):
+        for ref, value in zip(fresh[1:], gas_update(now, down, up, west, east)[1:]):
             ref[at : at + 8, :] = value
     sub2 = lax.broadcasted_iota(jnp.int32, (8, 2 * LANES), 0)
     lane2 = lax.broadcasted_iota(jnp.int32, (8, 2 * LANES), 1)
@@ -822,31 +928,17 @@
                 east.append(right)
             target = slice(0, LANES) if end == 0 else slice(width - LANES, width)
             kept = slice(0, LANES) if end == 0 else slice(LANES, 2 * LANES)
-            for ref, value in zip(fresh, gas_update(now, down, up, west, east)):
+            for ref, value in zip(fresh[1:], gas_update(now, down, up, west, east)[1:]):
                 ref[span, target] = value[:, kept]
         return _
 
     lax.fori_loop(1, blocks - 1, side_cells, 0)
 
-    finals = [
-        pltpu.make_async_copy(ref, final, field_sem.at[f])
-        for f, (ref, final) in enumerate(zip(fresh, (d_final, x_final, y_final)))
-    ]
-
-    for part in range(4):
-        for at in range(part * step1, (part + 1) * step1, 8):
-            for tile in range(width // LANES):
-                span = slice(tile * LANES, (tile + 1) * LANES)
-                near = d_out[at : at + 8, span]
-                far = d_out[at + packed : at + packed + 8, span]
-                src[2 * tile, at : at + 8, :] = jnp.where(low, near, flip(far))
-                src[2 * tile + 1, at : at + 8, :] = jnp.where(low, flip(near), far)
-        each(functools.partial(one, part), gy)
-    for final in finals:
+    for final in finals[1:]:
         final.start()
-    got1[azimuth] = src[azimuth]
     lax.fori_loop(0, outer, fill, 0)
-    table_load.wait()
+    for load in table_loads:
+        load.wait()
 
     for part in range(4):
         arrive(got1, recv1, step1, part)
@@ -971,7 +1063,8 @@
                     give4[a, at : at + 8, :] = even - odd
                     give4[gy - a, at : at + 8, :] = even + odd
         each(functools.partial(four, part), gy)
-    out[azimuth] = give4[azimuth]
+    own = pltpu.make_async_copy(give4.at[azimuth], out.at[azimuth], own_sem)
+    own.start()
     for final in finals:
         final.wait()
     for side in range(2):
@@ -983,6 +1076,7 @@
     for part in range(4):
         arrive(out, recv4, step1, part)
     leave(give4, send4)
+    own.wait()
 
 
 def fused_step(shift, fields, tables, nx, ny, gx, gy, ident):
@@ -1000,16 +1094,17 @@
     return pl.pallas_call(
         functools.partial(fused_kernel, nx, ny),
         out_shape=(shape, shape, shape, jax.ShapeDtypeStruct(blocks, f32)),
-        in_specs=[pl.BlockSpec(memory_space=pltpu.SMEM)]
-        + [VMEM] * 3
-        + [pl.BlockSpec(memory_space=pl.ANY)]
-        + [VMEM] * (len(tables) - 1),
-        out_specs=(pl.BlockSpec(memory_space=pl.ANY),) * 3 + (VMEM,),
-        scratch_shapes=[pltpu.VMEM((height, width), f32)] * 3
+        in_specs=[HBM] * 7,
+        out_specs=(HBM,) * 4,
+        scratch_shapes=[pltpu.SMEM((1,), jnp.int32)]
+        + [pltpu.VMEM((height, width), f32)] * 6
+        + [pltpu.VMEM(table.shape, table.dtype) for table in tables]
         + [
-            pltpu.VMEM(tables[0].shape, tables[0].dtype),
             pltpu.SemaphoreType.DMA,
             pltpu.SemaphoreType.DMA((3,)),
+            pltpu.SemaphoreType.DMA((3,)),
+            pltpu.SemaphoreType.DMA((3,)),
+            pltpu.SemaphoreType.DMA,
             pltpu.VMEM((2, gy, 8, height), f32),
             pltpu.VMEM((2, 8, width), f32),
             pltpu.VMEM((2, 8, height), f32),

time: 75 us -> 71.1 us (0.948)
  Pallas kernels: 73.6 us -> 69.6 us
    pallas_call x1, Pallas kernels: 70.6 us -> 67 us  [fused_step(): pl.pallas_call(functools.partial(fused_kernel, nx, ny), out_shape=(shape,...]
where the time goes in v2:
time: 71.1 us; the launch traced here: 70.9 us
  Pallas kernels  69.6 us (98%)
  between operations  1.29 us (2%)
    pallas_call x1, Pallas kernels, fused_step(): pl.pallas_call(functools.partial(fused_kernel, nx, ny), out_shape=(shape,...  67 us
    pallas_call x1, Pallas kernels, unpack(): pl.pallas_call(unpack_kernel, out_shape=(shape,) * 4, in_specs=[HBM] * 4,...  2.62 us

profile of v2, /device:TPU:0, one launch (start us, length us, event | category | flops | bytes accessed | tf_op | source)
XLA Modules:
  0.0 70.9 jit_solution(6304230914863813230)
XLA Ops:
  1.3 67.0 %shard_map.102 = (f32[128,1024]{1,0:T(8,128)}, f32[128,1024]{1,0:T(8,128)}, f32[128,1024]{1,0:T(8,128)}, f32[16,64,128]{2,1,0:T(8,128)}) custom-call(s32[1]{0:T(128)S(6)} %copy.11.shift_in, f32[128,1024]{1,0:T(8,128)} %bitcast.7, f32[128,1024]{1,0:T(8,128)} %bitcast.8, f32[128,1024]{1,0:T(8,128)} %bitcast.9, ...), custom_call_target="tpu_custom_call" | custom-call | tf_op jit(solution)/shard_map/pallas_call | solution.py:1094
  68.3 2.6 %shard_map.103 = (f32[128,1024]{1,0:T(8,128)}, f32[128,1024]{1,0:T(8,128)}, f32[128,1024]{1,0:T(8,128)}, f32[128,1024]{1,0:T(8,128)}) custom-call(f32[128,1024]{1,0:T(8,128)} %get-tuple-element.12.d_in, f32[128,1024]{1,0:T(8,128)} %get-tuple-element.13.x_in, f32[128,1024]{1,0:T(8,128)} %get-tuple-element.14.y_in, f32[16,64,128]{2,1,0:T(8,128)} %get-tuple-element.15.src_in), custom_call_target="tpu_custom_call" | custom-call | tf_op jit(solution)/shard_map/pallas_call | solution.py:292

commit v3 on v2

--- a/solution.py
+++ b/solution.py
@@ -812,6 +812,36 @@
 
     for side in range(2):
         row_copy(side).wait_recv()
+    for block in (0, blocks - 1):
+        at = block * 8
+        edge_down = [ref[at - 1 : at, :] if block else rows[0, f : f + 1, :] for f, ref in enumerate(fields)]
+        edge_up = [ref[at + 8 : at + 9, :] if block == 0 else rows[1, f : f + 1, :] for f, ref in enumerate(fields)]
+        density_rows(slice(at, at + 8), edge_down, edge_up)
+    def pack(peer, at):
+        span = slice(peer // 2 * LANES, (peer // 2 + 1) * LANES)
+        near = d_out[at : at + 8, span]
+        far = d_out[at + packed : at + packed + 8, span]
+        src[peer, at : at + 8, :] = jnp.where(low, flip(near) if peer % 2 else near, far if peer % 2 else flip(far))
+
+    ends = (0, gy - 1)
+    for part in range(4):
+        for at in range(part * step1, (part + 1) * step1, 8):
+            for peer in range(1, gy - 1):
+                pack(peer, at)
+
+        def send(k, _):
+            peer = lax.rem(azimuth + k, gy)
+
+            @pl.when(jnp.logical_and(peer != ends[0], peer != ends[1]))
+            def _middle():
+                one(part, k).start()
+
+            return _
+
+        lax.fori_loop(gy // 2, gy, send, 0)
+        lax.fori_loop(1, gy // 2, send, 0)
+
+    for side in range(2):
         col_wait(side, outer_edge if side == 0 else inner_edge, crecv)
     here = azimuth * height
 
@@ -828,11 +858,6 @@
         axis=0,
     ).T
     colbuf2[...] = ghost
-    for block in (0, blocks - 1):
-        at = block * 8
-        edge_down = [ref[at - 1 : at, :] if block else rows[0, f : f + 1, :] for f, ref in enumerate(fields)]
-        edge_up = [ref[at + 8 : at + 9, :] if block == 0 else rows[1, f : f + 1, :] for f, ref in enumerate(fields)]
-        density_rows(slice(at, at + 8), edge_down, edge_up)
     lane_tile = lax.broadcasted_iota(jnp.int32, (height, LANES), 1)
     for end in range(2):
         span = slice(0, LANES) if end == 0 else slice(width - LANES, width)
@@ -846,20 +871,21 @@
         flux = jnp.where(lane_tile == (0 if end == 0 else LANES - 1), time_step * flux, 0.0)
         d_out[:, span] = d_out[:, span] + flux if end == 0 else d_out[:, span] - flux
 
+    for at in range(0, packed, 8):
+        for end in ends:
+            pack(end, at)
+    for end in ends:
+
+        @pl.when(azimuth != end)
+        def _end():
+            for part in range(4):
+                one(part, lax.rem(end - azimuth + gy, gy)).start()
+
     finals = [
         pltpu.make_async_copy(ref, final, field_sem.at[f])
         for f, (ref, final) in enumerate(zip(fresh, (d_final, x_final, y_final)))
     ]
 
-    for part in range(4):
-        for at in range(part * step1, (part + 1) * step1, 8):
-            for tile in range(width // LANES):
-                span = slice(tile * LANES, (tile + 1) * LANES)
-                near = d_out[at : at + 8, span]
-                far = d_out[at + packed : at + packed + 8, span]
-                src[2 * tile, at : at + 8, :] = jnp.where(low, near, flip(far))
-                src[2 * tile + 1, at : at + 8, :] = jnp.where(low, flip(near), far)
-        each(functools.partial(one, part), gy)
     finals[0].start()
     got1[azimuth] = src[azimuth]
 

time: 71.1 us -> 67.9 us (0.955)
  Pallas kernels: 69.6 us -> 66.4 us
    pallas_call x1, Pallas kernels: 67 us -> 63.8 us  [fused_step(): pl.pallas_call(functools.partial(fused_kernel, nx, ny), out_shape=(shape,...]
where the time goes in v3:
time: 67.9 us; the launch traced here: 67.7 us
  Pallas kernels  66.4 us (98%)
  between operations  1.29 us (2%)
    pallas_call x1, Pallas kernels, fused_step(): pl.pallas_call(functools.partial(fused_kernel, nx, ny), out_shape=(shape,...  63.8 us
    pallas_call x1, Pallas kernels, unpack(): pl.pallas_call(unpack_kernel, out_shape=(shape,) * 4, in_specs=[HBM] * 4,...  2.62 us

profile of v3, /device:TPU:0, one launch (start us, length us, event | category | flops | bytes accessed | tf_op | source)
XLA Modules:
  0.0 67.7 jit_solution(1048169509502480534)
XLA Ops:
  1.3 63.8 %shard_map.102 = (f32[128,1024]{1,0:T(8,128)}, f32[128,1024]{1,0:T(8,128)}, f32[128,1024]{1,0:T(8,128)}, f32[16,64,128]{2,1,0:T(8,128)}) custom-call(s32[1]{0:T(128)S(6)} %copy.11.shift_in, f32[128,1024]{1,0:T(8,128)} %bitcast.7, f32[128,1024]{1,0:T(8,128)} %bitcast.8, f32[128,1024]{1,0:T(8,128)} %bitcast.9, ...), custom_call_target="tpu_custom_call" | custom-call | tf_op jit(solution)/shard_map/pallas_call | solution.py:1120
  65.1 2.6 %shard_map.103 = (f32[128,1024]{1,0:T(8,128)}, f32[128,1024]{1,0:T(8,128)}, f32[128,1024]{1,0:T(8,128)}, f32[128,1024]{1,0:T(8,128)}) custom-call(f32[128,1024]{1,0:T(8,128)} %get-tuple-element.12.d_in, f32[128,1024]{1,0:T(8,128)} %get-tuple-element.13.x_in, f32[128,1024]{1,0:T(8,128)} %get-tuple-element.14.y_in, f32[16,64,128]{2,1,0:T(8,128)} %get-tuple-element.15.src_in), custom_call_target="tpu_custom_call" | custom-call | tf_op jit(solution)/shard_map/pallas_call | solution.py:292

commit v4 on v3

--- a/solution.py
+++ b/solution.py
@@ -37,6 +37,27 @@
         return lax.dot_general(a, b, (dims, ((), ())), preferred_element_type=jnp.float32)
 
     return one(left[0], right[0]) + (one(left[0], right[1]) + one(left[1], right[0]))
+
+
+def dot_wide(table, value, dims):
+    def one(a, b):
+        return lax.dot_general(a, b, (dims, ((), ())), preferred_element_type=jnp.float32)
+
+    head, tail = split(value)
+    both = one(table[0], jnp.concatenate([head, tail], axis=1))
+    return both[:, :LANES] + (both[:, LANES:] + one(table[1], head))
+
+
+def dot_square(value, table):
+    both = jnp.dot(jnp.concatenate(split(value), axis=1), table, preferred_element_type=jnp.float32)
+    return both[:, :LANES] + both[:, LANES:]
+
+
+def square_np(table):
+    def one(head, tail):
+        return np.block([[head, tail], [head, np.zeros_like(tail)]])
+
+    return np.stack([one(table[0], table[1]), one(table[0].T, table[1].T)])
 
 
 def exchange_kernel(count, gy, whole, src, dst, send, recv, own):
@@ -262,28 +283,23 @@
     )(*fields, rows, cols)
 
 
-def unpack_kernel(d_in, x_in, y_in, src_in, d_out, x_out, y_out, out, d, x, y, src, packed_out, get, put):
+def unpack_kernel(d_in, x_in, y_in, src, d_out, x_out, y_out, out, packed_out, sem):
     gy, packed, _ = src.shape
     low = lax.broadcasted_iota(jnp.int32, (packed, LANES), 1) < LANES // 2
-    sources, buffers, targets = (src_in, d_in, x_in, y_in), (src, d, x, y), (out, d_out, x_out, y_out)
-    gets = [pltpu.make_async_copy(a, b, get.at[f]) for f, (a, b) in enumerate(zip(sources, buffers))]
-    puts = [
-        pltpu.make_async_copy(a, b, put.at[f])
-        for f, (a, b) in enumerate(zip((packed_out,) + buffers[1:], targets))
+    copies = [
+        pltpu.make_async_copy(source, target, sem.at[f])
+        for f, (source, target) in enumerate(zip((d_in, x_in, y_in), (d_out, x_out, y_out)))
     ]
-    for copy in gets:
+    copies.append(pltpu.make_async_copy(packed_out, out, sem.at[3]))
+    for copy in copies[:3]:
         copy.start()
-    gets[0].wait()
     for tile in range(gy // 2):
         span = slice(tile * LANES, (tile + 1) * LANES)
         near, far = src[2 * tile], src[2 * tile + 1]
         packed_out[0:packed, span] = jnp.where(low, near, flip(far))
         packed_out[packed : 2 * packed, span] = jnp.where(low, flip(near), far)
-    puts[0].start()
-    for f in range(1, 4):
-        gets[f].wait()
-        puts[f].start()
-    for copy in puts:
+    copies[3].start()
+    for copy in copies:
         copy.wait()
 
 
@@ -292,11 +308,10 @@
     return pl.pallas_call(
         unpack_kernel,
         out_shape=(shape,) * 4,
-        in_specs=[HBM] * 4,
+        in_specs=[HBM] * 3 + [VMEM],
         out_specs=(HBM,) * 4,
-        scratch_shapes=[pltpu.VMEM(fields[0].shape, jnp.float32)] * 3
-        + [pltpu.VMEM(blocks.shape, jnp.float32), pltpu.VMEM(fields[0].shape, jnp.float32)]
-        + [pltpu.SemaphoreType.DMA((4,))] * 2,
+        scratch_shapes=[pltpu.VMEM(fields[0].shape, jnp.float32), pltpu.SemaphoreType.DMA((4,))],
+        compiler_params=pltpu.CompilerParams(vmem_limit_bytes=8 << 20),
     )(*fields, blocks)
 
 
@@ -995,7 +1010,7 @@
     lane = lax.broadcasted_iota(jnp.int32, (height, LANES), 1)
     ratio = height // lines
     for g in range(half_gy):
-        both = dot3((y_table[0, g], y_table[1, g]), split(stage[g]), ((1,), (0,)))
+        both = dot_wide((y_table[0, g], y_table[1, g]), stage[g], ((1,), (0,)))
         value = jnp.where(lane < wide, both[:height], flip(both[height:]))
         for q in range(ratio):
             give2[g * ratio + q] = value[q * lines : (q + 1) * lines]
@@ -1014,9 +1029,9 @@
         for n in range(outer):
             value = turned(parts[n], ci, -si)
             mid[n] = turned(value, turn[0, n : n + 1, :], turn[1, n : n + 1, :])
-        modes = dot3(split(mid[...].reshape(outer * 8, LANES)), (x_table[0], x_table[1]), ((1,), (0,)))
+        modes = dot_square(mid[...].reshape(outer * 8, LANES), x_table[0])
         modes = modes * green[:, rows, :].reshape(outer * 8, LANES)
-        modes = dot3(split(modes), (x_table[0], x_table[1]), ((1,), (1,)))
+        modes = dot_square(modes, x_table[1])
         mid[...] = modes.reshape(outer, 8, LANES)
         parts = []
         for n in range(outer):
@@ -1062,7 +1077,7 @@
     for g in range(half_gy):
         value = got3[g * ratio : (g + 1) * ratio].reshape(height, LANES)
         value = jnp.concatenate([value, flip(value)], axis=0)
-        stage[g] = dot3((y_table[0, g], y_table[1, g]), split(value), ((0,), (0,)))
+        stage[g] = dot_wide((y_table[0, g], y_table[1, g]), value, ((0,), (0,)))
 
     def take(group, base, at):
         near = stage[group, base + at : base + at + 8, :]
@@ -1120,7 +1135,7 @@
     return pl.pallas_call(
         functools.partial(fused_kernel, nx, ny),
         out_shape=(shape, shape, shape, jax.ShapeDtypeStruct(blocks, f32)),
-        in_specs=[HBM] * 7,
+        in_specs=[pl.BlockSpec(memory_space=pltpu.HBM)] * 7,
         out_specs=(HBM,) * 4,
         scratch_shapes=[pltpu.SMEM((1,), jnp.int32)]
         + [pltpu.VMEM((height, width), f32)] * 6
@@ -1151,8 +1166,10 @@
             pltpu.VMEM(blocks, f32),
         ]
         + sems,
-        compiler_params=pltpu.CompilerParams(collective_id=ident, has_side_effects=True),
-    )(shift, *fields, *tables)
+        compiler_params=pltpu.CompilerParams(
+            collective_id=ident, has_side_effects=True, vmem_limit_bytes=28 << 20
+        ),
+    )(shift, *[pltpu.with_memory_space_constraint(a, pltpu.HBM) for a in (*fields, *tables)])
 
 
 def shards(density, xmomentum, ymomentum, shear_shift):
@@ -1173,9 +1190,10 @@
     group = wide // xb
     y_table = jnp.asarray(azimuth_table(gy, height))
     turn, table = radial_tables(nx)
+    square = jnp.asarray(square_np(table))
     turn, table = jnp.asarray(turn), jnp.asarray(table)
     if group == 1 and packed % 32 == 0 and lines % 8 == 0 and height % lines == 0:
-        results = fused_step(shear_shift, fields, (y_table, turn, table), nx, ny, gx, gy, 1)
+        results = fused_step(shear_shift, fields, (y_table, turn, square), nx, ny, gx, gy, 1)
         return tuple(r[None] for r in unpack(results[:3], results[3]))
 
     cols, rows = halo(fields, gx, gy, 0)

time: 67.9 us -> 66.1 us (0.973)
  Pallas kernels: 66.4 us -> 64.6 us
    pallas_call x1, Pallas kernels: 2.62 us -> 1.35 us  [unpack(): pl.pallas_call(unpack_kernel, out_shape=(shape,) * 4, in_specs=[HBM] * 3...]
where the time goes in v4:
time: 66.1 us; the launch traced here: 65.9 us
  Pallas kernels  64.6 us (98%)
  between operations  1.29 us (2%)
    pallas_call x1, Pallas kernels, fused_step(): pl.pallas_call(functools.partial(fused_kernel, nx, ny), out_shape=(shape,...  63.3 us
    pallas_call x1, Pallas kernels, unpack(): pl.pallas_call(unpack_kernel, out_shape=(shape,) * 4, in_specs=[HBM] * 3...  1.35 us

profile of v4, /device:TPU:0, one launch (start us, length us, event | category | flops | bytes accessed | tf_op | source)
XLA Modules:
  0.0 65.9 jit_solution(9595841189315865788)
XLA Ops:
  1.3 63.3 %shard_map.102 = (f32[128,1024]{1,0:T(8,128)S(1)}, f32[128,1024]{1,0:T(8,128)S(1)}, f32[128,1024]{1,0:T(8,128)S(1)}, f32[16,64,128]{2,1,0:T(8,128)S(1)}) custom-call(s32[1]{0:T(128)S(6)} %copy.11.shift_in, f32[128,1024]{1,0:T(8,128)} %bitcast.7, f32[128,1024]{1,0:T(8,128)} %bitcast.8, f32[128,1024]{1,0:T(8,128)} %bitcast.9, ...), custom_call_target="tpu_custom_call" | custom-call | tf_op jit(solution)/shard_map/pallas_call | solution.py:1135
  64.6 1.3 %shard_map.103 = (f32[128,1024]{1,0:T(8,128)}, f32[128,1024]{1,0:T(8,128)}, f32[128,1024]{1,0:T(8,128)}, f32[128,1024]{1,0:T(8,128)}) custom-call(f32[128,1024]{1,0:T(8,128)S(1)} %get-tuple-element.12.d_in, f32[128,1024]{1,0:T(8,128)S(1)} %get-tuple-element.13.x_in, f32[128,1024]{1,0:T(8,128)S(1)} %get-tuple-element.14.y_in, ...), custom_call_target="tpu_custom_call" | custom-call | tf_op jit(solution)/shard_map/pallas_call | solution.py:308
